TPU v7x, 32 devices: a whole 2x2x4 slice. The times are simulated.
32 devices in a mesh: wide: 16 (over z, x, core), narrow: 2 (over y).
Axes of the slice: x: 2, y: 2, z: 4, core: 2. Of those that a mesh axis runs over, the one named last changes fastest.
Arguments:
- layer_in: bfloat16 [128, 256, 768], P(('wide', 'narrow')), may hold values from -6 to 6
- segment_ids: int32 [128, 256], P(('wide', 'narrow')), may hold values from 0 to 31, as said below
- live_mask: int32 [128, 256], P(('wide', 'narrow')), may hold values from 0 to 1, as said below
- expert_ids: int32 [128], P(('wide', 'narrow')), may hold values from 1 to 2
- cotangent: bfloat16 [128, 256, 768], P(('wide', 'narrow')), may hold values from -6 to 6
- norm1_gain: float32 [768], replicated, may hold values from 0.1 to 1.9
- norm1_bias: float32 [768], replicated, may hold values from -3 to 3
- q_weight: bfloat16 [768, 768], P('wide'), may hold values from -0.21875 to 0.21875
- q_bias: float32 [768], replicated, may hold values from -3 to 3
- k_weight: bfloat16 [768, 768], P('wide'), may hold values from -0.21875 to 0.21875
- v_weight: bfloat16 [768, 768], P('wide'), may hold values from -0.21875 to 0.21875
- v_bias: float32 [768], replicated, may hold values from -3 to 3
- o_weight: bfloat16 [768, 768], P('wide'), may hold values from -0.875 to 0.875
- o_bias: float32 [768], replicated, may hold values from -3 to 3
- norm2_gain: float32 [768], replicated, may hold values from 0.1 to 1.9
- norm2_bias: float32 [768], replicated, may hold values from -3 to 3
- in_weight: bfloat16 [768, 3072], P('wide'), may hold values from -0.21875 to 0.21875
- in_bias: float32 [3072], replicated, may hold values from -3 to 3
- out_weight: bfloat16 [3072, 768], P('wide'), may hold values from -0.109375 to 0.109375
- out_bias: float32 [768], replicated, may hold values from -3 to 3
Outputs:
- layer_out: bfloat16 [128, 256, 768], P(('wide', 'narrow'))
- input_grad: bfloat16 [128, 256, 768], P(('wide', 'narrow'))
- counts: int32 [3], replicated
- norm1_gain_grad: float32 [768], replicated
- norm1_bias_grad: float32 [768], replicated
- q_weight_grad: float32 [768, 768], P('wide')
- q_bias_grad: float32 [768], replicated
- k_weight_grad: float32 [768, 768], P('wide')
- v_weight_grad: float32 [768, 768], P('wide')
- v_bias_grad: float32 [768], replicated
- o_weight_grad: float32 [768, 768], P('wide')
- o_bias_grad: float32 [768], replicated
- norm2_gain_grad: float32 [768], replicated
- norm2_bias_grad: float32 [768], replicated
- in_weight_grad: float32 [768, 3072], P('wide')
- in_bias_grad: float32 [3072], replicated
- out_weight_grad: float32 [3072, 768], P('wide')
- out_bias_grad: float32 [768], replicated
Inputs may be any that keep to these rules, and one draw needn't show every extreme that they name: `segment_ids`: in each row the captions, 8 to 40 tokens each, lie in order and are numbered from 0; after the last caption the padding slots carry the next number. `live_mask`: the live slots of a row are a prefix of it, at least 8 of them. `expert_ids`: no row names the vision expert.
All inputs are finite; a program needn't handle non-finite values.
Results may differ from a plain program's by a relative error of at most 0.018.
Values may be sent and summed in bfloat16 or wider, within the bound.
A program may use at most 192 MiB of HBM per device.

v0:
```python
import math
import jax
import jax.numpy as jnp
from jax import lax
from jax.sharding import PartitionSpec as P

HEADS = 12
EPSILON = 1e-06
MASKED = -1e30


def norm_rows(values, gain_vec, bias_vec):
    row_mean = jnp.mean(values, axis=-1, keepdims=True)
    centred = values - row_mean
    variance = jnp.mean(centred * centred, axis=-1, keepdims=True)
    return centred * lax.rsqrt(variance + EPSILON) * gain_vec + bias_vec


def gelu_exact(values):
    return jax.nn.gelu(values, approximate=False)


def plain_product(left, right):
    return jnp.dot(left, right, preferred_element_type=jnp.float32)


def product_left_t(left, right):
    return lax.dot_general(
        left, right, (((0,), (0,)), ((), ())), preferred_element_type=jnp.float32
    )


def product_right_t(left, right):
    return lax.dot_general(
        left, right, (((1,), (1,)), ((), ())), preferred_element_type=jnp.float32
    )


def allowed_pairs(seg_rows, live_rows):
    slot_total = seg_rows.shape[-1]
    row_pos = lax.broadcasted_iota(jnp.int32, (slot_total, slot_total), 0)
    col_pos = lax.broadcasted_iota(jnp.int32, (slot_total, slot_total), 1)
    same_seg = seg_rows[:, :, None] == seg_rows[:, None, :]
    return (same_seg & ((live_rows[:, None, :] > 0) | (row_pos == col_pos)[None]))[:, None]


def masked_scores(query_heads, key_heads, seg_rows, live_rows):
    raw_scores = (
        jnp.einsum("gqhe,gkhe->ghqk", query_heads, key_heads, preferred_element_type=jnp.float32)
        * 0.125
    )
    return jnp.where(allowed_pairs(seg_rows, live_rows), raw_scores, MASKED)


def attend_block(pieces):
    query_heads, key_heads, value_heads, seg_rows, live_rows = pieces
    scores = masked_scores(query_heads, key_heads, seg_rows, live_rows)
    row_top = jnp.max(scores, axis=-1, keepdims=True)
    exp_terms = jnp.exp(scores - row_top)
    row_total = jnp.sum(exp_terms, axis=-1, keepdims=True)
    attn_probs = (exp_terms / row_total).astype(jnp.bfloat16)
    mixed_heads = jnp.einsum(
        "ghqk,gkhe->gqhe", attn_probs, value_heads, preferred_element_type=jnp.float32
    )
    return (mixed_heads.astype(jnp.bfloat16), row_top + jnp.log(row_total))


def attend_back(pieces):
    query_heads, key_heads, value_heads, seg_rows, live_rows, log_total, grad_mixed = pieces
    scores = masked_scores(query_heads, key_heads, seg_rows, live_rows)
    attn_probs = jnp.exp(scores - log_total)
    grad_probs = jnp.einsum(
        "gqhe,gkhe->ghqk", grad_mixed, value_heads, preferred_element_type=jnp.float32
    )
    inner_sum = jnp.sum(grad_probs * attn_probs, axis=-1, keepdims=True)
    grad_scores = (attn_probs * (grad_probs - inner_sum)).astype(jnp.bfloat16)
    grad_query = (
        jnp.einsum("ghqk,gkhe->gqhe", grad_scores, key_heads, preferred_element_type=jnp.float32)
        * 0.125
    ).astype(jnp.bfloat16)
    grad_keys = (
        jnp.einsum("ghqk,gqhe->gkhe", grad_scores, query_heads, preferred_element_type=jnp.float32)
        * 0.125
    ).astype(jnp.bfloat16)
    grad_values = jnp.einsum(
        "ghqk,gqhe->gkhe",
        attn_probs.astype(jnp.bfloat16),
        grad_mixed,
        preferred_element_type=jnp.float32,
    ).astype(jnp.bfloat16)
    return (grad_query, grad_keys, grad_values)


def body(
    layer_in,
    segment_ids,
    live_mask,
    expert_ids,
    cotangent,
    norm1_gain,
    norm1_bias,
    q_weight,
    q_bias,
    k_weight,
    v_weight,
    v_bias,
    o_weight,
    o_bias,
    norm2_gain,
    norm2_bias,
    in_weight,
    in_bias,
    out_weight,
    out_bias,
):
    row_local, slot_total, width_all = layer_in.shape
    head_dim = width_all // HEADS
    group_rows = math.gcd(row_local, max(1, 512 // slot_total))
    block_total = row_local // group_rows
    token_total = row_local * slot_total
    live_tokens = jnp.sum(live_mask, axis=1)
    local_counts = jnp.stack(
        [jnp.sum(jnp.where(expert_ids == expert, live_tokens, 0)) for expert in range(3)]
    )
    counts = lax.psum(local_counts, ("wide", "narrow"))
    count_float = counts.astype(jnp.float32)
    own_count = jnp.where(expert_ids == 1, count_float[1], count_float[2])
    row_scale = (count_float[1] + count_float[2]) / (2.0 * own_count)

    def heads_blocks(values):
        return values.reshape(block_total, group_rows, slot_total, HEADS, head_dim)

    seg_blocks = segment_ids.reshape(block_total, group_rows, slot_total)
    live_blocks = live_mask.reshape(block_total, group_rows, slot_total)
    x_rows = layer_in.astype(jnp.float32).reshape(token_total, width_all)
    normed_one = norm_rows(x_rows, norm1_gain, norm1_bias).astype(jnp.bfloat16)
    full_q, full_k, full_v, full_o = (
        lax.all_gather(q_weight, "wide", axis=0, tiled=True),
        lax.all_gather(k_weight, "wide", axis=0, tiled=True),
        lax.all_gather(v_weight, "wide", axis=0, tiled=True),
        lax.all_gather(o_weight, "wide", axis=0, tiled=True),
    )
    query_act = (plain_product(normed_one, full_q) + q_bias).astype(jnp.bfloat16)
    key_act = plain_product(normed_one, full_k).astype(jnp.bfloat16)
    value_act = (plain_product(normed_one, full_v) + v_bias).astype(jnp.bfloat16)
    mixed_blocks, log_total = lax.map(
        attend_block,
        (
            heads_blocks(query_act),
            heads_blocks(key_act),
            heads_blocks(value_act),
            seg_blocks,
            live_blocks,
        ),
    )
    mixed_act = mixed_blocks.reshape(token_total, width_all)
    residual = x_rows + plain_product(mixed_act, full_o) + o_bias
    normed_two = norm_rows(residual, norm2_gain, norm2_bias).astype(jnp.bfloat16)
    full_in, full_out = (
        lax.all_gather(in_weight, "wide", axis=0, tiled=True),
        lax.all_gather(out_weight, "wide", axis=0, tiled=True),
    )
    pre_act = plain_product(normed_two, full_in) + in_bias
    hidden = gelu_exact(pre_act).astype(jnp.bfloat16)
    result = residual + plain_product(hidden, full_out) + out_bias
    layer_out = result.astype(jnp.bfloat16).reshape(row_local, slot_total, width_all)
    token_scale = (live_mask.astype(jnp.float32) * row_scale[:, None]).reshape(token_total, 1)
    grad_y = cotangent.astype(jnp.float32).reshape(token_total, width_all) * token_scale
    grad_branch = grad_y.astype(jnp.bfloat16)
    back_in, back_out = (
        lax.all_gather(in_weight, "wide", axis=0, tiled=True),
        lax.all_gather(out_weight, "wide", axis=0, tiled=True),
    )
    grad_hidden = product_right_t(grad_branch, back_out)
    gelu_pull = jax.vjp(gelu_exact, pre_act)[1]
    grad_pre = gelu_pull(grad_hidden)[0].astype(jnp.bfloat16)
    out_weight_grad = product_left_t(hidden, grad_branch)
    out_bias_grad = jnp.sum(grad_branch.astype(jnp.float32), axis=0)
    in_weight_grad = product_left_t(normed_two, grad_pre)
    in_bias_grad = jnp.sum(grad_pre.astype(jnp.float32), axis=0)
    grad_normed_two = product_right_t(grad_pre, back_in)
    norm_two_pull = jax.vjp(norm_rows, residual, norm2_gain, norm2_bias)[1]
    grad_resid_norm, norm2_gain_grad, norm2_bias_grad = norm_two_pull(grad_normed_two)
    grad_resid = grad_y + grad_resid_norm
    grad_attn = grad_resid.astype(jnp.bfloat16)
    back_q, back_k, back_v, back_o = (
        lax.all_gather(q_weight, "wide", axis=0, tiled=True),
        lax.all_gather(k_weight, "wide", axis=0, tiled=True),
        lax.all_gather(v_weight, "wide", axis=0, tiled=True),
        lax.all_gather(o_weight, "wide", axis=0, tiled=True),
    )
    o_weight_grad = product_left_t(mixed_act, grad_attn)
    o_bias_grad = jnp.sum(grad_attn.astype(jnp.float32), axis=0)
    grad_mixed = product_right_t(grad_attn, back_o).astype(jnp.bfloat16)
    grad_query, grad_keys, grad_values = lax.map(
        attend_back,
        (
            heads_blocks(query_act),
            heads_blocks(key_act),
            heads_blocks(value_act),
            seg_blocks,
            live_blocks,
            log_total,
            heads_blocks(grad_mixed),
        ),
    )
    grad_query = grad_query.reshape(token_total, width_all)
    grad_keys = grad_keys.reshape(token_total, width_all)
    grad_values = grad_values.reshape(token_total, width_all)
    q_weight_grad = product_left_t(normed_one, grad_query)
    q_bias_grad = jnp.sum(grad_query.astype(jnp.float32), axis=0)
    k_weight_grad = product_left_t(normed_one, grad_keys)
    v_weight_grad = product_left_t(normed_one, grad_values)
    v_bias_grad = jnp.sum(grad_values.astype(jnp.float32), axis=0)
    grad_normed_one = (
        product_right_t(grad_query, back_q)
        + product_right_t(grad_keys, back_k)
        + product_right_t(grad_values, back_v)
    )
    norm_one_pull = jax.vjp(norm_rows, x_rows, norm1_gain, norm1_bias)[1]
    grad_x_norm, norm1_gain_grad, norm1_bias_grad = norm_one_pull(grad_normed_one)
    input_grad = (
        (grad_resid + grad_x_norm).astype(jnp.bfloat16).reshape(row_local, slot_total, width_all)
    )
    summed_vectors = lax.psum(
        (
            norm1_gain_grad,
            norm1_bias_grad,
            q_bias_grad,
            v_bias_grad,
            o_bias_grad,
            norm2_gain_grad,
            norm2_bias_grad,
            in_bias_grad,
            out_bias_grad,
        ),
        ("wide", "narrow"),
    )
    row_pieces = (
        lax.psum_scatter(
            q_weight_grad.astype(jnp.bfloat16), "wide", scatter_dimension=0, tiled=True
        ).astype(jnp.float32),
        lax.psum_scatter(
            k_weight_grad.astype(jnp.bfloat16), "wide", scatter_dimension=0, tiled=True
        ).astype(jnp.float32),
        lax.psum_scatter(
            v_weight_grad.astype(jnp.bfloat16), "wide", scatter_dimension=0, tiled=True
        ).astype(jnp.float32),
        lax.psum_scatter(
            o_weight_grad.astype(jnp.bfloat16), "wide", scatter_dimension=0, tiled=True
        ).astype(jnp.float32),
        lax.psum_scatter(
            in_weight_grad.astype(jnp.bfloat16), "wide", scatter_dimension=0, tiled=True
        ).astype(jnp.float32),
        lax.psum_scatter(
            out_weight_grad.astype(jnp.bfloat16), "wide", scatter_dimension=0, tiled=True
        ).astype(jnp.float32),
    )
    row_pieces = (
        lax.psum(row_pieces[0].astype(jnp.bfloat16), "narrow").astype(jnp.float32),
        lax.psum(row_pieces[1].astype(jnp.bfloat16), "narrow").astype(jnp.float32),
        lax.psum(row_pieces[2].astype(jnp.bfloat16), "narrow").astype(jnp.float32),
        lax.psum(row_pieces[3].astype(jnp.bfloat16), "narrow").astype(jnp.float32),
        lax.psum(row_pieces[4].astype(jnp.bfloat16), "narrow").astype(jnp.float32),
        lax.psum(row_pieces[5].astype(jnp.bfloat16), "narrow").astype(jnp.float32),
    )
    return (
        layer_out,
        input_grad,
        counts,
        summed_vectors[0],
        summed_vectors[1],
        row_pieces[0],
        summed_vectors[2],
        row_pieces[1],
        row_pieces[2],
        summed_vectors[3],
        row_pieces[3],
        summed_vectors[4],
        summed_vectors[5],
        summed_vectors[6],
        row_pieces[4],
        summed_vectors[7],
        row_pieces[5],
        summed_vectors[8],
    )


def solution(mesh):
    placed = (
        P(("wide", "narrow"), None, None),
        P(("wide", "narrow"), None),
        P(("wide", "narrow"), None),
        P(("wide", "narrow")),
        P(("wide", "narrow"), None, None),
        P(),
        P(),
        P("wide", None),
        P(),
        P("wide", None),
        P("wide", None),
        P(),
        P("wide", None),
        P(),
        P(),
        P(),
        P("wide", None),
        P(),
        P("wide", None),
        P(),
    )
    return jax.shard_map(
        body,
        mesh=mesh,
        in_specs=placed,
        out_specs=(
            P(("wide", "narrow"), None, None),
            P(("wide", "narrow"), None, None),
            P(),
            P(),
            P(),
            P("wide", None),
            P(),
            P("wide", None),
            P("wide", None),
            P(),
            P("wide", None),
            P(),
            P(),
            P(),
            P("wide", None),
            P(),
            P("wide", None),
            P(),
        ),
        check_vma=False,
    )
```

profile of v0, /device:TPU:0, one launch (start us, length us, event | category | flops | bytes accessed | tf_op | source)
XLA Modules:
  0.0 776.0 jit_solution(13493928599702478998)
XLA Ops:
  18.4 42.4 %psum.112 = s32[3]{0:T(128)S(1)} all-reduce(s32[3]{0:T(128)S(1)} %pad_add_fusion), channel_id=1, replica_groups=mesh['wide'=16,'narrow'=2] {'wide','narrow'}, use_global_device_ids=true, to_apply=%region_12.13 | all-reduce | flops 3 | bytes 24 | tf_op jit(solution)/shard_map/psum | solution.py:125
  68.3 3.8 add_convert_fusion.5
  76.4 14.6 %all-gather.9.cloned.1.call-done = bf16[768,768]{1,0:T(8,128)(2,1)} async-done(((bf16[48,768]{1,0:T(8,128)(2,1)}), bf16[768,768]{1,0:T(8,128)(2,1)}) %all-gather.9.cloned.1.call-update) | async-done | bytes 1179664 | tf_op jit(solution)/shard_map/all_gather | solution.py:138
  91.0 2.7 add_convert_fusion.4
  94.4 2.4 reshape.312
  98.5 32.1 %all-gather.11.cloned.1.call-done = bf16[768,768]{1,0:T(8,128)(2,1)} async-done(((bf16[48,768]{1,0:T(8,128)(2,1)}), bf16[768,768]{1,0:T(8,128)(2,1)}) %all-gather.11.cloned.1.call-update) | async-done | bytes 1179664 | tf_op jit(solution)/shard_map/all_gather | solution.py:139
  130.6 4.3 convolution_convert_fusion.3
  134.9 2.6 copy.55
  137.5 3.8 reshape.313
  141.3 2.9 copy.58
  146.4 16.6 %while.26 = (s32[]{:T(128)}, bf16[2,2,256,12,64]{2,1,0,4,3:T(2,128)(2,1)}, f32[2,2,12,256,1]{3,2,1,4,0:T(8,128)}, bf16[2,2,256,12,64]{2,4,3,1,0:T(8,128)(2,1)}, ...) while((s32[]{:T(128)}, ...), condition=%wide.region_5.6_spmd, body=%wide.region_2.5_spmd.sunk | while | flops 422373888 | bytes 30772356 | solution.py:146
  147.1 2.3 fusion.151
  155.1 2.4 fusion.151
  163.0 3.8 reshape.314
  166.8 3.3 all-gather.13.cloned.1.call-done
  170.1 3.9 fusion.94
  176.2 48.2 %all-gather.15.cloned.1.call-done = bf16[768,3072]{1,0:T(8,128)(2,1)} async-done(((bf16[48,3072]{1,0:T(8,128)(2,1)}), bf16[768,3072]{1,0:T(8,128)(2,1)}) %all-gather.15.cloned.1.call-update) | async-done | bytes 4718608 | tf_op jit(solution)/shard_map/all_gather | solution.py:160
  224.4 38.2 %multiply_convert_fusion.3 = (bf16[1024,3072]{1,0:T(8,128)(2,1)}, f32[1024,3072]{1,0:T(8,128)}, f32[1024,3072]{1,0:T(8,128)}) fusion(f32[3072]{0:T(1024)S(1)} %copy-done.55, bf16[768,3072]{1,0:T(8,128)(2,1)} %all-gather.15.cloned.1.call-done, f32[1024,768]{1,0:T(8,128)} %copy-done.12, f32[768]{0:T(1024)S(1)} %copy-done.59, f32[768]{0:T(1024)S(1)} %copy-done.48, ...), kind=kOutput, calls=%fused_computation.74 | convolution fusion | flops 5043388416 | bytes 39348224 | tf_op jit(solution)/shard_map/dot_general | solution.py:24
  262.6 15.8 %all-gather.17.cloned.1.call-done = bf16[3072,768]{1,0:T(8,128)(2,1)} async-done(((bf16[192,768]{1,0:T(8,128)(2,1)}), bf16[3072,768]{1,0:T(8,128)(2,1)}) %all-gather.17.cloned.1.call-update) | async-done | bytes 4718608 | tf_op jit(solution)/shard_map/all_gather | solution.py:161
  278.4 19.0 %convert_reduce_fusion = (f32[3072]{0:T(1024)}, bf16[1024,3072]{1,0:T(8,128)(2,1)}) fusion(f32[1024,3072]{1,0:T(8,128)} %get-tuple-element.231, bf16[1024,768]{1,0:T(8,128)(2,1)} %fusion.76, bf16[3072,768]{1,0:T(8,128)(2,1)} %all-gather.17.cloned.1.call-done, f32[1024,3072]{1,0:T(8,128)} %get-tuple-element.244, f32[3072]{0:T(1024)S(1)} %copy-done.55), kind=kOutput, calls=%fused_computation.72 | convolution fusion | flops 4885312512 | bytes 37773312 | tf_op jit(solution)/shard_map/dot_general | solution.py:34
  297.4 10.2 %multiply_reduce_fusion.1 = (f32[768]{0:T(1024)}, f32[1024]{0:T(1024)S(1)}, f32[768]{0:T(1024)}, f32[1024,768]{1,0:T(8,128)S(1)}) fusion(f32[1024,768]{1,0:T(8,128)S(1)} %copy-done.13, f32[1024]{0:T(1024)S(1)} %fusion.78, f32[1024]{0:T(1024)S(1)} %broadcast_multiply_fusion, f32[768]{0:T(1024)S(1)} %copy-done.48, ...), kind=kOutput, calls=%fused_computation.115 | convolution fusion | flops 4838126592 | bytes 17323008 | tf_op jit(solution)/shard_map/dot_general | solution.py:34
  312.6 2.4 convolution_convert_fusion.4
  315.0 4.0 convolution_convert_fusion.2
  319.1 2.6 copy.60
  321.6 3.9 reshape.317
  327.7 30.1 %while.27 = (s32[]{:T(128)}, bf16[2,2,256,12,64]{2,4,3,1,0:T(8,128)(2,1)}, bf16[2,2,256,12,64]{2,1,0,4,3:T(2,128)(2,1)}, bf16[2,2,256,12,64]{2,4,3,1,0:T(8,128)(...) while((s32[]{:T(128)}, ...), condition=%wide.region_17.18_spmd, body=%wide.region_15.17_spmd.sunk | while | flops 1032645120 | bytes 109375376 | solution.py:195
  340.3 2.5 fusion.165
  355.3 2.5 fusion.165
  357.8 3.0 copy.67
  362.2 4.4 convolution_convert_fusion.5
  368.3 2.4 reshape.318
  370.7 4.6 convolution_convert_fusion.7
  375.4 2.3 reshape.319
  377.7 4.5 convolution_convert_fusion.6
  382.3 10.0 %convolution_convert_fusion.1 = bf16[768,3072]{1,0:T(8,128)(2,1)} fusion(bf16[1024,3072]{1,0:T(8,128)(2,1)} %get-tuple-element.248, f32[1024,768]{1,0:T(8,128)S(1)} %copy-done.14, f32[768]{0:T(1024)S(1)} %copy-done.60, f32[768]{0:T(1024)S(1)} %copy-done.48, f32[1024]{0:T(1024)S(1)} %fusion.78, f32[1024]{0:T(1024)S(1)} %broadcast_multiply_fusion), kind=kOutput, calls=%fused_computation.89 | convolution fusion | flops 4838129664 | bytes 14170112 | tf_op jit(solution)/shard_map/dot_general | solution.py:28
  393.7 9.9 %convolution_convert_fusion = bf16[3072,768]{1,0:T(8,128)(2,1)} fusion(bf16[1024,3072]{1,0:T(8,128)(2,1)} %get-tuple-element.230, bf16[1024,768]{1,0:T(8,128)(2,1)S(1)} %copy-done.24), kind=kOutput, calls=%fused_computation.88 | convolution fusion | flops 4834197504 | bytes 12582912 | tf_op jit(solution)/shard_map/dot_general | solution.py:28
  405.6 2.9 fusion.95
  410.7 3.7 fusion.89
  414.4 3.2 fusion.69
  417.6 6.1 add_convert_fusion.2
  423.8 8.8 %reduce-scatter.11.cloned.1.call-done = bf16[48,768]{1,0:T(8,128)(2,1)} async-done(((bf16[768,768]{1,0:T(8,128)(2,1)}), bf16[48,768]{1,0:T(8,128)(2,1)}) %reduce-scatter.11.cloned.1.call-update) | async-done | bytes 73744 | tf_op jit(solution)/shard_map/reduce_scatter | solution.py:246
  432.5 60.8 %reduce-scatter.7.cloned.1.call-done = bf16[48,768]{1,0:T(8,128)(2,1)} async-done(((bf16[768,768]{1,0:T(8,128)(2,1)}), bf16[48,768]{1,0:T(8,128)(2,1)}) %reduce-scatter.7.cloned.1.call-update) | async-done | bytes 73744 | tf_op jit(solution)/shard_map/reduce_scatter | solution.py:240
  493.3 60.5 %reduce-scatter.9.cloned.1.call-done = bf16[48,768]{1,0:T(8,128)(2,1)} async-done(((bf16[768,768]{1,0:T(8,128)(2,1)}), bf16[48,768]{1,0:T(8,128)(2,1)}) %reduce-scatter.9.cloned.1.call-update) | async-done | bytes 73744 | tf_op jit(solution)/shard_map/reduce_scatter | solution.py:243
  553.8 78.6 %reduce-scatter.15.cloned.1.call-done = bf16[48,3072]{1,0:T(8,128)(2,1)} async-done(((bf16[768,3072]{1,0:T(8,128)(2,1)}), bf16[48,3072]{1,0:T(8,128)(2,1)}) %reduce-scatter.15.cloned.1.call-update) | async-done | bytes 294928 | tf_op jit(solution)/shard_map/reduce_scatter | solution.py:252
  632.3 78.9 %reduce-scatter.17.cloned.1.call-done = bf16[192,768]{1,0:T(8,128)(2,1)} async-done(((bf16[3072,768]{1,0:T(8,128)(2,1)}), bf16[192,768]{1,0:T(8,128)(2,1)}) %reduce-scatter.17.cloned.1.call-update) | async-done | bytes 294928 | tf_op jit(solution)/shard_map/reduce_scatter | solution.py:255
  711.2 2.4 convert_reduce_fusion.4
  713.7 41.2 %all-reduce = (f32[768]{0:T(1024)}, f32[768]{0:T(1024)}, f32[768]{0:T(1024)}, f32[768]{0:T(1024)}, f32[768]{0:T(1024)}, /*index=5*/f32[768]{0:T(1024)}, f32[768]{0:T(1024)}, f32[3072]{0:T(1024)}, f32[768]{0:T(1024)}) all-reduce(f32[768]{0:T(1024)S(1)} %get-tuple-element.165, ...), channel_id=1, replica_groups=mesh['wide'=16,'narrow'=2] {'wide','narrow'}, use_global_device_ids=true, to_apply=%region_21.22 | all-reduce | flops 9216 | bytes 73728 | tf_op jit(solution)/shard_map/psum | solution.py:225
  754.9 4.5 add_convert_fusion.1
  (277 shorter events, 90.2 us)
Async XLA Ops:
  7.2 56.8 %copy-start.38 = (s32[4,256]{1,0:T(4,128)S(1)}, s32[4,256]{1,0:T(4,128)}, u32[]{:S(2)}) copy-start(s32[4,256]{1,0:T(4,128)} %param.26) | copy-start | bytes 12292
  7.2 7.3 copy-start.3
  7.2 8.5 %copy-start.52 = (s32[4]{0:T(128)S(1)}, s32[4]{0:T(128)}, u32[]{:S(2)}) copy-start(s32[4]{0:T(128)} %param.27) | copy-start | bytes 52
  7.2 11.2 %copy-start.49 = (s32[4,256]{1,0:T(4,128)S(1)}, s32[4,256]{1,0:T(4,128)}, u32[]{:S(2)}) copy-start(s32[4,256]{1,0:T(4,128)} %param.25) | copy-start | bytes 12292
  7.2 56.9 %copy-start.32 = (f32[768]{0:T(1024)S(1)}, f32[768]{0:T(1024)}, u32[]{:S(2)}) copy-start(f32[768]{0:T(1024)} %param.29) | copy-start | bytes 9220
  7.2 56.9 %copy-start.44 = (f32[768]{0:T(1024)S(1)}, f32[768]{0:T(1024)}, u32[]{:S(2)}) copy-start(f32[768]{0:T(1024)} %param.30) | copy-start | bytes 9220
  7.3 61.0 %all-gather.7.cloned.1.call-start = ((), (), s32[]{:S(2)}) async-start(), calls=%async_computation.6 | async-start | bytes 1253376 | tf_op jit(solution)/shard_map/all_gather | solution.py:140
  8.0 83.0 %all-gather.9.cloned.1.call-start = ((), (), s32[]{:S(2)}) async-start(), calls=%async_computation.7 | async-start | bytes 1253376 | tf_op jit(solution)/shard_map/all_gather | solution.py:138
  8.7 121.9 %all-gather.11.cloned.1.call-start = ((), (), s32[]{:S(2)}) async-start(), calls=%async_computation.8 | async-start | bytes 1253376 | tf_op jit(solution)/shard_map/all_gather | solution.py:139
  9.5 160.6 %all-gather.13.cloned.1.call-start = ((), (), s32[]{:S(2)}) async-start(), calls=%async_computation.9 | async-start | bytes 1253376 | tf_op jit(solution)/shard_map/all_gather | solution.py:141
  10.1 214.4 %all-gather.15.cloned.1.call-start = ((), (), s32[]{:S(2)}) async-start(), calls=%async_computation.10 | async-start | bytes 5013504 | tf_op jit(solution)/shard_map/all_gather | solution.py:160
  10.6 267.7 %all-gather.17.cloned.1.call-start = ((), (), s32[]{:S(2)}) async-start(), calls=%async_computation.11 | async-start | bytes 5013504 | tf_op jit(solution)/shard_map/all_gather | solution.py:161
  11.2 412.6 %reduce-scatter.13.cloned.1.call-start = ((), (), s32[]{:S(2)}) async-start(), calls=%async_computation.15 | async-start | bytes 1253376 | tf_op jit(solution)/shard_map/reduce_scatter | solution.py:249
  15.7 50.9 %copy-start.36 = (f32[1024]{0:T(1024)}, f32[1024]{0:T(1024)S(1)}, u32[]{:S(2)}) copy-start(f32[1024]{0:T(1024)S(1)} %rsqrt.25) | copy-start | bytes 12292
  15.7 50.9 %copy-start.34 = (f32[1,2,4,128]{3,1,2,0:T(2,128)}, f32[1,2,4,128]{3,1,2,0:T(2,128)S(1)}, u32[]{:S(2)}) copy-start(f32[1,2,4,128]{3,1,2,0:T(2,128)S(1)} %copy.77) | copy-start | bytes 12292
  66.6 5.5 copy-start.28
  73.8 17.2 %copy-start.57 = (f32[768]{0:T(1024)S(1)}, f32[768]{0:T(1024)}, u32[]{:S(2)}) copy-start(f32[768]{0:T(1024)} %param.32) | copy-start | bytes 9220
  75.0 16.0 %copy-start.29 = (bf16[1024,768]{1,0:T(8,128)(2,1)S(1)}, bf16[1024,768]{1,0:T(8,128)(2,1)}, u32[]{:S(2)}) copy-start(bf16[1024,768]{1,0:T(8,128)(2,1)} %copy-done.28) | copy-start | bytes 4718596
  163.0 7.1 copy-start.58
  174.0 50.4 %copy-start.48 = (f32[768]{0:T(1024)S(1)}, f32[768]{0:T(1024)}, u32[]{:S(2)}) copy-start(f32[768]{0:T(1024)} %param.38) | copy-start | bytes 9220
  174.0 50.4 %copy-start.55 = (f32[3072]{0:T(1024)S(1)}, f32[3072]{0:T(1024)}, u32[]{:S(2)}) copy-start(f32[3072]{0:T(1024)} %param.41) | copy-start | bytes 36868
  174.0 50.4 %copy-start.59 = (f32[768]{0:T(1024)S(1)}, f32[768]{0:T(1024)}, u32[]{:S(2)}) copy-start(f32[768]{0:T(1024)} %param.39) | copy-start | bytes 9220
  278.4 19.0 %copy-start.13 = (f32[1024,768]{1,0:T(8,128)S(1)}, f32[1024,768]{1,0:T(8,128)}, u32[]{:S(2)}) copy-start(f32[1024,768]{1,0:T(8,128)} %copy-done.12) | copy-start | bytes 9437188
  307.6 3.2 copy-start.41
  315.0 117.6 %reduce-scatter.11.cloned.1.call-start = ((), (), s32[]{:S(2)}) async-start(), calls=%async_computation.14 | async-start | bytes 1253376 | tf_op jit(solution)/shard_map/reduce_scatter | solution.py:246
  328.0 3.8 copy-start.10
  343.0 3.8 copy-start.10
  362.2 4.5 copy-start.22
  362.2 4.5 copy-start.18
  366.7 126.7 %reduce-scatter.7.cloned.1.call-start = ((), (), s32[]{:S(2)}) async-start(), calls=%async_computation.12 | async-start | bytes 1253376 | tf_op jit(solution)/shard_map/reduce_scatter | solution.py:240
  370.7 4.6 copy-start.21
  375.3 178.5 %reduce-scatter.9.cloned.1.call-start = ((), (), s32[]{:S(2)}) async-start(), calls=%async_computation.13 | async-start | bytes 1253376 | tf_op jit(solution)/shard_map/reduce_scatter | solution.py:243
  377.7 4.6 copy-start.14
  377.7 4.6 copy-start.60
  382.2 250.1 %reduce-scatter.15.cloned.1.call-start = ((), (), s32[]{:S(2)}) async-start(), calls=%async_computation.16 | async-start | bytes 5013504 | tf_op jit(solution)/shard_map/reduce_scatter | solution.py:252
  392.3 318.9 %reduce-scatter.17.cloned.1.call-start = ((), (), s32[]{:S(2)}) async-start(), calls=%async_computation.17 | async-start | bytes 5013504 | tf_op jit(solution)/shard_map/reduce_scatter | solution.py:255
  403.7 355.7 %all-reduce.4.cloned.1.call-start = ((), (), s32[]{:S(2)}) async-start(), calls=%async_computation.18 | async-start | bytes 1769472 | tf_op jit(solution)/shard_map/psum | solution.py:260
  408.5 9.1 %slice-start = ((s8[4718592]{0:T(1024)(128)(4,1)}), s8[4194304]{0:T(1024)(128)(4,1)S(1)}, s32[]{:S(2)}) async-start(s8[4718592]{0:T(1024)(128)(4,1)} %bitcast.232), calls=%async_computation.19 | async-start | bytes 8388608
  408.5 9.1 %slice-start.2 = ((s8[6291456]{0:T(1024)(128)(4,1)}), s8[4194304]{0:T(1024)(128)(4,1)S(1)}, s32[]{:S(2)}) async-start(s8[6291456]{0:T(1024)(128)(4,1)} %bitcast.235), calls=%async_computation.21 | async-start | bytes 8388608
  410.7 3.7 copy-start.43
  410.7 3.7 copy-start.37
  410.7 6.9 slice-start.1
  410.7 6.9 slice-start.3
  414.4 3.2 copy-start.15
  414.4 3.2 copy-start.61
  423.8 290.0 %copy-start.45 = (f32[3072]{0:T(1024)S(1)}, f32[3072]{0:T(1024)}, u32[]{:S(2)}) copy-start(f32[3072]{0:T(1024)} %get-tuple-element.247) | copy-start | bytes 36868
  423.8 290.0 %copy-start.50 = (f32[768]{0:T(1024)S(1)}, f32[768]{0:T(1024)}, u32[]{:S(2)}) copy-start(f32[768]{0:T(1024)} %get-tuple-element.163) | copy-start | bytes 9220
  423.8 290.0 %copy-start.51 = (f32[768]{0:T(1024)S(1)}, f32[768]{0:T(1024)}, u32[]{:S(2)}) copy-start(f32[768]{0:T(1024)} %get-tuple-element.167) | copy-start | bytes 9220
  (42 other events, 84.1 us)
Sparse Core Ops, SparseCore 0:
  10.4 41.0 all-gather.6
  53.7 37.2 all-gather.8
  93.3 37.2 all-gather.10
  132.8 37.2 all-gather.12
  172.2 52.1 all-gather.14
  226.6 51.7 all-gather.16
  315.1 56.6 reduce-scatter.12
  375.4 57.1 reduce-scatter.10
  436.2 57.1 reduce-scatter.6
  496.8 56.9 reduce-scatter.8
  557.6 74.6 reduce-scatter.14
  636.5 74.6 reduce-scatter.16
  713.9 36.9 all-reduce.3
where the time goes:
time: 785 us; the launch traced here: 776 us
  waiting for transfers between devices  405 us (52%)
  matrix products  162 us (21%)
  blocking collectives  83.6 us (11%)
  local copies, waits for them, and re-layouts  65.2 us (8%)
  other arithmetic  42.9 us (5%)
  between operations  16.1 us (2%)
    reduce_scatter x1, waiting for transfers between devices, body(): lax.psum_scatter(out_weight_grad.astype(jnp.bfloat16), 'wide', scatter_di...  78.9 us
    reduce_scatter x1, waiting for transfers between devices, body(): lax.psum_scatter(in_weight_grad.astype(jnp.bfloat16), 'wide', scatter_dim...  78.6 us
    reduce_scatter x1, waiting for transfers between devices, body(): lax.psum_scatter(q_weight_grad.astype(jnp.bfloat16), 'wide', scatter_dime...  60.8 us
    reduce_scatter x1, waiting for transfers between devices, body(): lax.psum_scatter(k_weight_grad.astype(jnp.bfloat16), 'wide', scatter_dime...  60.5 us
    dot_general x6, matrix products, plain_product(): return jnp.dot(left, right, preferred_element_type=jnp.float32)  59 us
    all_gather x1, waiting for transfers between devices, body(): lax.all_gather(in_weight, 'wide', axis=0, tiled=True)  48.2 us
    psum x1, blocking collectives, body(): counts = lax.psum(local_counts, ('wide', 'narrow'))  42.4 us
    dot_general x6, matrix products, product_right_t(): lax.dot_general(left, right, (((1,), (1,)), ((), ())), preferred_element_...  41.2 us
  transfers between devices with their start and end apart: 13, of which 10 were waited for; matrix products, arithmetic and copies ran while one was open for 28% of the time, Pallas kernels for 0%

commit v1 on v0

--- a/solution.py
+++ b/solution.py
@@ -222,7 +222,7 @@
     input_grad = (
         (grad_resid + grad_x_norm).astype(jnp.bfloat16).reshape(row_local, slot_total, width_all)
     )
-    summed_vectors = lax.psum(
+    half = lax.psum(
         (
             norm1_gain_grad,
             norm1_bias_grad,
@@ -234,8 +234,9 @@
             in_bias_grad,
             out_bias_grad,
         ),
-        ("wide", "narrow"),
-    )
+        "narrow",
+    )
+    summed_vectors = lax.psum(half, "wide")
     row_pieces = (
         lax.psum_scatter(
             q_weight_grad.astype(jnp.bfloat16), "wide", scatter_dimension=0, tiled=True

time: 785 us -> 811 us (1.033)
  blocking collectives: 83.6 us -> 110 us
    psum x0 -> x1, blocking collectives: none -> 58.4 us  [body(): summed_vectors = lax.psum(half, 'wide')]
    psum x1, blocking collectives: 41.2 us -> 8.98 us  [body(): lax.psum((norm1_gain_grad, norm1_bias_grad, q_bias_grad, v_bias_grad, o_b...]
  transfers between devices with their start and end apart: 13 -> 13, of which waited for: 10 -> 10; matrix products, arithmetic and copies ran while one was open for 28% -> 27% of each run, Pallas kernels for 0% -> 0%
where the time goes in v1:
time: 811 us; the launch traced here: 802 us
  waiting for transfers between devices  405 us (50%)
  matrix products  162 us (20%)
  blocking collectives  110 us (14%)
  local copies, waits for them, and re-layouts  65.1 us (8%)
  other arithmetic  42.9 us (5%)
  between operations  16.1 us (2%)
    reduce_scatter x1, waiting for transfers between devices, body(): lax.psum_scatter(out_weight_grad.astype(jnp.bfloat16), 'wide', scatter_di...  78.9 us
    reduce_scatter x1, waiting for transfers between devices, body(): lax.psum_scatter(in_weight_grad.astype(jnp.bfloat16), 'wide', scatter_dim...  78.5 us
    reduce_scatter x1, waiting for transfers between devices, body(): lax.psum_scatter(q_weight_grad.astype(jnp.bfloat16), 'wide', scatter_dime...  60.7 us
    reduce_scatter x1, waiting for transfers between devices, body(): lax.psum_scatter(k_weight_grad.astype(jnp.bfloat16), 'wide', scatter_dime...  60.5 us
    dot_general x6, matrix products, plain_product(): return jnp.dot(left, right, preferred_element_type=jnp.float32)  59 us
    psum x1, blocking collectives, body(): summed_vectors = lax.psum(half, 'wide')  58.4 us
    all_gather x1, waiting for transfers between devices, body(): lax.all_gather(in_weight, 'wide', axis=0, tiled=True)  48.2 us
    psum x1, blocking collectives, body(): counts = lax.psum(local_counts, ('wide', 'narrow'))  42.4 us
  transfers between devices with their start and end apart: 13, of which 10 were waited for; matrix products, arithmetic and copies ran while one was open for 27% of the time, Pallas kernels for 0%

profile of v1, /device:TPU:0, one launch (start us, length us, event | category | flops | bytes accessed | tf_op | source)
XLA Modules:
  0.0 802.1 jit_solution(15726784548656234792)
XLA Ops:
  18.4 42.4 %psum.175 = s32[3]{0:T(128)S(1)} all-reduce(s32[3]{0:T(128)S(1)} %pad_add_fusion), channel_id=1, replica_groups=mesh['wide'=16,'narrow'=2] {'wide','narrow'}, use_global_device_ids=true, to_apply=%region_12.13 | all-reduce | flops 3 | bytes 24 | tf_op jit(solution)/shard_map/psum | solution.py:125
  68.3 3.8 add_convert_fusion.5
  76.5 14.6 %all-gather.9.cloned.1.call-done = bf16[768,768]{1,0:T(8,128)(2,1)} async-done(((bf16[48,768]{1,0:T(8,128)(2,1)}), bf16[768,768]{1,0:T(8,128)(2,1)}) %all-gather.9.cloned.1.call-update) | async-done | bytes 1179664 | tf_op jit(solution)/shard_map/all_gather | solution.py:138
  91.0 2.7 add_convert_fusion.4
  94.5 2.4 reshape.312
  98.5 32.1 %all-gather.11.cloned.1.call-done = bf16[768,768]{1,0:T(8,128)(2,1)} async-done(((bf16[48,768]{1,0:T(8,128)(2,1)}), bf16[768,768]{1,0:T(8,128)(2,1)}) %all-gather.11.cloned.1.call-update) | async-done | bytes 1179664 | tf_op jit(solution)/shard_map/all_gather | solution.py:139
  130.6 4.3 convolution_convert_fusion.3
  134.9 2.6 copy.55
  137.5 3.8 reshape.313
  141.3 2.9 copy.58
  146.4 16.5 %while.26 = (s32[]{:T(128)}, bf16[2,2,256,12,64]{2,1,0,4,3:T(2,128)(2,1)}, f32[2,2,12,256,1]{3,2,1,4,0:T(8,128)}, bf16[2,2,256,12,64]{2,4,3,1,0:T(8,128)(2,1)}, ...) while((s32[]{:T(128)}, ...), condition=%wide.region_5.6_spmd, body=%wide.region_2.5_spmd.sunk | while | flops 422373888 | bytes 30772356 | solution.py:146
  155.2 2.4 fusion.151
  163.0 3.8 reshape.314
  166.8 3.3 all-gather.13.cloned.1.call-done
  170.1 3.9 fusion.94
  176.2 48.2 %all-gather.15.cloned.1.call-done = bf16[768,3072]{1,0:T(8,128)(2,1)} async-done(((bf16[48,3072]{1,0:T(8,128)(2,1)}), bf16[768,3072]{1,0:T(8,128)(2,1)}) %all-gather.15.cloned.1.call-update) | async-done | bytes 4718608 | tf_op jit(solution)/shard_map/all_gather | solution.py:160
  224.4 38.2 %multiply_convert_fusion.3 = (bf16[1024,3072]{1,0:T(8,128)(2,1)}, f32[1024,3072]{1,0:T(8,128)}, f32[1024,3072]{1,0:T(8,128)}) fusion(f32[3072]{0:T(1024)S(1)} %copy-done.55, bf16[768,3072]{1,0:T(8,128)(2,1)} %all-gather.15.cloned.1.call-done, f32[1024,768]{1,0:T(8,128)} %copy-done.12, f32[768]{0:T(1024)S(1)} %copy-done.59, f32[768]{0:T(1024)S(1)} %copy-done.48, ...), kind=kOutput, calls=%fused_computation.74 | convolution fusion | flops 5043388416 | bytes 39348224 | tf_op jit(solution)/shard_map/dot_general | solution.py:24
  262.6 15.8 %all-gather.17.cloned.1.call-done = bf16[3072,768]{1,0:T(8,128)(2,1)} async-done(((bf16[192,768]{1,0:T(8,128)(2,1)}), bf16[3072,768]{1,0:T(8,128)(2,1)}) %all-gather.17.cloned.1.call-update) | async-done | bytes 4718608 | tf_op jit(solution)/shard_map/all_gather | solution.py:161
  278.4 18.9 %convert_reduce_fusion = (f32[3072]{0:T(1024)}, bf16[1024,3072]{1,0:T(8,128)(2,1)}) fusion(f32[1024,3072]{1,0:T(8,128)} %get-tuple-element.240, bf16[1024,768]{1,0:T(8,128)(2,1)} %fusion.76, bf16[3072,768]{1,0:T(8,128)(2,1)} %all-gather.17.cloned.1.call-done, f32[1024,3072]{1,0:T(8,128)} %get-tuple-element.253, f32[3072]{0:T(1024)S(1)} %copy-done.55), kind=kOutput, calls=%fused_computation.72 | convolution fusion | flops 4885312512 | bytes 37773312 | tf_op jit(solution)/shard_map/dot_general | solution.py:34
  297.2 10.2 %multiply_reduce_fusion.1 = (f32[768]{0:T(1024)}, f32[1024]{0:T(1024)S(1)}, f32[768]{0:T(1024)}, f32[1024,768]{1,0:T(8,128)S(1)}) fusion(f32[1024,768]{1,0:T(8,128)S(1)} %copy-done.13, f32[1024]{0:T(1024)S(1)} %fusion.78, f32[1024]{0:T(1024)S(1)} %broadcast_multiply_fusion, f32[768]{0:T(1024)S(1)} %copy-done.48, ...), kind=kOutput, calls=%fused_computation.115 | convolution fusion | flops 4838126592 | bytes 17323008 | tf_op jit(solution)/shard_map/dot_general | solution.py:34
  312.4 2.4 convolution_convert_fusion.4
  314.9 4.0 convolution_convert_fusion.2
  318.9 2.6 copy.60
  321.5 3.9 reshape.317
  327.5 30.1 %while.27 = (s32[]{:T(128)}, bf16[2,2,256,12,64]{2,4,3,1,0:T(8,128)(2,1)}, bf16[2,2,256,12,64]{2,1,0,4,3:T(2,128)(2,1)}, bf16[2,2,256,12,64]{2,4,3,1,0:T(8,128)(...) while((s32[]{:T(128)}, ...), condition=%wide.region_17.18_spmd, body=%wide.region_15.17_spmd.sunk | while | flops 1032645120 | bytes 109375376 | solution.py:195
  340.1 2.5 fusion.165
  355.1 2.5 fusion.165
  357.6 3.0 copy.67
  362.0 4.5 convolution_convert_fusion.5
  368.1 2.4 reshape.318
  370.5 4.5 convolution_convert_fusion.7
  375.1 2.3 reshape.319
  377.5 4.5 convolution_convert_fusion.6
  382.0 10.0 %convolution_convert_fusion.1 = bf16[768,3072]{1,0:T(8,128)(2,1)} fusion(bf16[1024,3072]{1,0:T(8,128)(2,1)} %get-tuple-element.257, f32[1024,768]{1,0:T(8,128)S(1)} %copy-done.14, f32[768]{0:T(1024)S(1)} %copy-done.60, f32[768]{0:T(1024)S(1)} %copy-done.48, f32[1024]{0:T(1024)S(1)} %fusion.78, f32[1024]{0:T(1024)S(1)} %broadcast_multiply_fusion), kind=kOutput, calls=%fused_computation.89 | convolution fusion | flops 4838129664 | bytes 14170112 | tf_op jit(solution)/shard_map/dot_general | solution.py:28
  393.4 10.0 %convolution_convert_fusion = bf16[3072,768]{1,0:T(8,128)(2,1)} fusion(bf16[1024,3072]{1,0:T(8,128)(2,1)} %get-tuple-element.239, bf16[1024,768]{1,0:T(8,128)(2,1)S(1)} %copy-done.24), kind=kOutput, calls=%fused_computation.88 | convolution fusion | flops 4834197504 | bytes 12582912 | tf_op jit(solution)/shard_map/dot_general | solution.py:28
  405.4 2.9 fusion.95
  410.5 3.7 fusion.89
  414.2 3.2 fusion.69
  417.5 6.1 add_convert_fusion.2
  423.6 8.8 %reduce-scatter.11.cloned.1.call-done = bf16[48,768]{1,0:T(8,128)(2,1)} async-done(((bf16[768,768]{1,0:T(8,128)(2,1)}), bf16[48,768]{1,0:T(8,128)(2,1)}) %reduce-scatter.11.cloned.1.call-update) | async-done | bytes 73744 | tf_op jit(solution)/shard_map/reduce_scatter | solution.py:247
  432.4 60.7 %reduce-scatter.7.cloned.1.call-done = bf16[48,768]{1,0:T(8,128)(2,1)} async-done(((bf16[768,768]{1,0:T(8,128)(2,1)}), bf16[48,768]{1,0:T(8,128)(2,1)}) %reduce-scatter.7.cloned.1.call-update) | async-done | bytes 73744 | tf_op jit(solution)/shard_map/reduce_scatter | solution.py:241
  493.1 60.5 %reduce-scatter.9.cloned.1.call-done = bf16[48,768]{1,0:T(8,128)(2,1)} async-done(((bf16[768,768]{1,0:T(8,128)(2,1)}), bf16[48,768]{1,0:T(8,128)(2,1)}) %reduce-scatter.9.cloned.1.call-update) | async-done | bytes 73744 | tf_op jit(solution)/shard_map/reduce_scatter | solution.py:244
  553.6 78.5 %reduce-scatter.15.cloned.1.call-done = bf16[48,3072]{1,0:T(8,128)(2,1)} async-done(((bf16[768,3072]{1,0:T(8,128)(2,1)}), bf16[48,3072]{1,0:T(8,128)(2,1)}) %reduce-scatter.15.cloned.1.call-update) | async-done | bytes 294928 | tf_op jit(solution)/shard_map/reduce_scatter | solution.py:253
  632.2 78.9 %reduce-scatter.17.cloned.1.call-done = bf16[192,768]{1,0:T(8,128)(2,1)} async-done(((bf16[3072,768]{1,0:T(8,128)(2,1)}), bf16[192,768]{1,0:T(8,128)(2,1)}) %reduce-scatter.17.cloned.1.call-update) | async-done | bytes 294928 | tf_op jit(solution)/shard_map/reduce_scatter | solution.py:256
  711.1 2.4 convert_reduce_fusion.4
  713.6 9.0 %all-reduce.1 = (f32[768]{0:T(1024)S(1)}, f32[768]{0:T(1024)S(1)}, f32[768]{0:T(1024)S(1)}, f32[768]{0:T(1024)S(1)}, f32[768]{0:T(1024)S(1)}, /*index=5*/f32[768...) all-reduce(f32[768]{0:T(1024)S(1)} %get-tuple-element.165, ...), channel_id=1, replica_groups=mesh['wide'=16,'narrow'=2] {'narrow'}, use_global_device_ids=true, to_apply=%region_21.22 | all-reduce | flops 9216 | bytes 73728 | tf_op jit(solution)/shard_map/psum | solution.py:225
  722.6 58.4 %all-reduce = (f32[768]{0:T(1024)}, f32[768]{0:T(1024)}, f32[768]{0:T(1024)}, f32[768]{0:T(1024)}, f32[768]{0:T(1024)}, /*index=5*/f32[768]{0:T(1024)}, f32[768]{0:T(1024)}, f32[3072]{0:T(1024)}, f32[768]{0:T(1024)}) all-reduce(f32[768]{0:T(1024)S(1)} %get-tuple-element.220, ...), channel_id=1, replica_groups=mesh['wide'=16,'narrow'=2] {'wide'}, use_global_device_ids=true, to_apply=%region_22.23 | all-reduce | flops 9216 | bytes 73728 | tf_op jit(solution)/shard_map/psum | solution.py:239
  781.0 4.5 add_convert_fusion.1
  (278 shorter events, 92.5 us)
Async XLA Ops:
  7.2 56.8 %copy-start.38 = (s32[4,256]{1,0:T(4,128)S(1)}, s32[4,256]{1,0:T(4,128)}, u32[]{:S(2)}) copy-start(s32[4,256]{1,0:T(4,128)} %param.26) | copy-start | bytes 12292
  7.2 7.3 copy-start.3
  7.2 8.5 %copy-start.52 = (s32[4]{0:T(128)S(1)}, s32[4]{0:T(128)}, u32[]{:S(2)}) copy-start(s32[4]{0:T(128)} %param.27) | copy-start | bytes 52
  7.2 11.2 %copy-start.49 = (s32[4,256]{1,0:T(4,128)S(1)}, s32[4,256]{1,0:T(4,128)}, u32[]{:S(2)}) copy-start(s32[4,256]{1,0:T(4,128)} %param.25) | copy-start | bytes 12292
  7.2 56.9 %copy-start.32 = (f32[768]{0:T(1024)S(1)}, f32[768]{0:T(1024)}, u32[]{:S(2)}) copy-start(f32[768]{0:T(1024)} %param.29) | copy-start | bytes 9220
  7.2 56.9 %copy-start.44 = (f32[768]{0:T(1024)S(1)}, f32[768]{0:T(1024)}, u32[]{:S(2)}) copy-start(f32[768]{0:T(1024)} %param.30) | copy-start | bytes 9220
  7.3 61.0 %all-gather.7.cloned.1.call-start = ((), (), s32[]{:S(2)}) async-start(), calls=%async_computation.6 | async-start | bytes 1253376 | tf_op jit(solution)/shard_map/all_gather | solution.py:140
  8.0 83.0 %all-gather.9.cloned.1.call-start = ((), (), s32[]{:S(2)}) async-start(), calls=%async_computation.7 | async-start | bytes 1253376 | tf_op jit(solution)/shard_map/all_gather | solution.py:138
  8.7 121.9 %all-gather.11.cloned.1.call-start = ((), (), s32[]{:S(2)}) async-start(), calls=%async_computation.8 | async-start | bytes 1253376 | tf_op jit(solution)/shard_map/all_gather | solution.py:139
  9.5 160.6 %all-gather.13.cloned.1.call-start = ((), (), s32[]{:S(2)}) async-start(), calls=%async_computation.9 | async-start | bytes 1253376 | tf_op jit(solution)/shard_map/all_gather | solution.py:141
  10.1 214.4 %all-gather.15.cloned.1.call-start = ((), (), s32[]{:S(2)}) async-start(), calls=%async_computation.10 | async-start | bytes 5013504 | tf_op jit(solution)/shard_map/all_gather | solution.py:160
  10.6 267.7 %all-gather.17.cloned.1.call-start = ((), (), s32[]{:S(2)}) async-start(), calls=%async_computation.11 | async-start | bytes 5013504 | tf_op jit(solution)/shard_map/all_gather | solution.py:161
  11.2 412.4 %reduce-scatter.13.cloned.1.call-start = ((), (), s32[]{:S(2)}) async-start(), calls=%async_computation.15 | async-start | bytes 1253376 | tf_op jit(solution)/shard_map/reduce_scatter | solution.py:250
  15.7 50.9 %copy-start.36 = (f32[1024]{0:T(1024)}, f32[1024]{0:T(1024)S(1)}, u32[]{:S(2)}) copy-start(f32[1024]{0:T(1024)S(1)} %rsqrt.25) | copy-start | bytes 12292
  15.7 50.9 %copy-start.34 = (f32[1,2,4,128]{3,1,2,0:T(2,128)}, f32[1,2,4,128]{3,1,2,0:T(2,128)S(1)}, u32[]{:S(2)}) copy-start(f32[1,2,4,128]{3,1,2,0:T(2,128)S(1)} %copy.77) | copy-start | bytes 12292
  66.6 5.5 copy-start.28
  73.8 17.2 %copy-start.57 = (f32[768]{0:T(1024)S(1)}, f32[768]{0:T(1024)}, u32[]{:S(2)}) copy-start(f32[768]{0:T(1024)} %param.32) | copy-start | bytes 9220
  75.0 16.0 %copy-start.29 = (bf16[1024,768]{1,0:T(8,128)(2,1)S(1)}, bf16[1024,768]{1,0:T(8,128)(2,1)}, u32[]{:S(2)}) copy-start(bf16[1024,768]{1,0:T(8,128)(2,1)} %copy-done.28) | copy-start | bytes 4718596
  163.0 7.1 copy-start.58
  174.0 50.4 %copy-start.48 = (f32[768]{0:T(1024)S(1)}, f32[768]{0:T(1024)}, u32[]{:S(2)}) copy-start(f32[768]{0:T(1024)} %param.38) | copy-start | bytes 9220
  174.0 50.4 %copy-start.55 = (f32[3072]{0:T(1024)S(1)}, f32[3072]{0:T(1024)}, u32[]{:S(2)}) copy-start(f32[3072]{0:T(1024)} %param.41) | copy-start | bytes 36868
  174.0 50.4 %copy-start.59 = (f32[768]{0:T(1024)S(1)}, f32[768]{0:T(1024)}, u32[]{:S(2)}) copy-start(f32[768]{0:T(1024)} %param.39) | copy-start | bytes 9220
  278.4 18.9 %copy-start.13 = (f32[1024,768]{1,0:T(8,128)S(1)}, f32[1024,768]{1,0:T(8,128)}, u32[]{:S(2)}) copy-start(f32[1024,768]{1,0:T(8,128)} %copy-done.12) | copy-start | bytes 9437188
  307.4 3.2 copy-start.41
  314.8 117.6 %reduce-scatter.11.cloned.1.call-start = ((), (), s32[]{:S(2)}) async-start(), calls=%async_computation.14 | async-start | bytes 1253376 | tf_op jit(solution)/shard_map/reduce_scatter | solution.py:247
  327.8 3.8 copy-start.10
  342.8 3.8 copy-start.10
  361.9 4.5 copy-start.22
  362.0 4.5 copy-start.18
  366.4 126.7 %reduce-scatter.7.cloned.1.call-start = ((), (), s32[]{:S(2)}) async-start(), calls=%async_computation.12 | async-start | bytes 1253376 | tf_op jit(solution)/shard_map/reduce_scatter | solution.py:241
  370.5 4.6 copy-start.21
  375.1 178.6 %reduce-scatter.9.cloned.1.call-start = ((), (), s32[]{:S(2)}) async-start(), calls=%async_computation.13 | async-start | bytes 1253376 | tf_op jit(solution)/shard_map/reduce_scatter | solution.py:244
  377.5 4.5 copy-start.14
  377.5 4.6 copy-start.60
  381.9 250.2 %reduce-scatter.15.cloned.1.call-start = ((), (), s32[]{:S(2)}) async-start(), calls=%async_computation.16 | async-start | bytes 5013504 | tf_op jit(solution)/shard_map/reduce_scatter | solution.py:253
  392.0 319.0 %reduce-scatter.17.cloned.1.call-start = ((), (), s32[]{:S(2)}) async-start(), calls=%async_computation.17 | async-start | bytes 5013504 | tf_op jit(solution)/shard_map/reduce_scatter | solution.py:256
  403.5 382.0 %all-reduce.5.cloned.1.call-start = ((), (), s32[]{:S(2)}) async-start(), calls=%async_computation.18 | async-start | bytes 1769472 | tf_op jit(solution)/shard_map/psum | solution.py:261
  408.3 9.1 %slice-start = ((s8[4718592]{0:T(1024)(128)(4,1)}), s8[4194304]{0:T(1024)(128)(4,1)S(1)}, s32[]{:S(2)}) async-start(s8[4718592]{0:T(1024)(128)(4,1)} %bitcast.232), calls=%async_computation.19 | async-start | bytes 8388608
  408.3 9.1 %slice-start.2 = ((s8[6291456]{0:T(1024)(128)(4,1)}), s8[4194304]{0:T(1024)(128)(4,1)S(1)}, s32[]{:S(2)}) async-start(s8[6291456]{0:T(1024)(128)(4,1)} %bitcast.235), calls=%async_computation.21 | async-start | bytes 8388608
  410.5 3.7 copy-start.43
  410.5 3.7 copy-start.37
  410.5 6.9 slice-start.1
  410.5 6.9 slice-start.3
  414.2 3.2 copy-start.15
  414.2 3.2 copy-start.61
  423.6 290.0 %copy-start.45 = (f32[3072]{0:T(1024)S(1)}, f32[3072]{0:T(1024)}, u32[]{:S(2)}) copy-start(f32[3072]{0:T(1024)} %get-tuple-element.256) | copy-start | bytes 36868
  423.6 290.0 %copy-start.50 = (f32[768]{0:T(1024)S(1)}, f32[768]{0:T(1024)}, u32[]{:S(2)}) copy-start(f32[768]{0:T(1024)} %get-tuple-element.163) | copy-start | bytes 9220
  423.6 290.0 %copy-start.51 = (f32[768]{0:T(1024)S(1)}, f32[768]{0:T(1024)}, u32[]{:S(2)}) copy-start(f32[768]{0:T(1024)} %get-tuple-element.167) | copy-start | bytes 9220
  (42 other events, 84.1 us)
Sparse Core Ops, SparseCore 0:
  10.4 41.0 all-gather.6
  53.7 37.2 all-gather.8
  93.3 37.2 all-gather.10
  132.8 37.2 all-gather.12
  172.2 52.1 all-gather.14
  226.6 51.7 all-gather.16
  314.9 56.6 reduce-scatter.12
  375.2 57.1 reduce-scatter.10
  436.0 57.0 reduce-scatter.6
  496.6 56.9 reduce-scatter.8
  557.5 74.6 reduce-scatter.14
  636.4 74.6 reduce-scatter.16
  713.7 36.4 all-reduce.4
